TPU v7x, 32 devices: a whole 2x2x4 slice. The times are simulated.
32 devices in a mesh: wide: 8 (over z, y), narrow: 4 (over x, core).
Axes of the slice: x: 2, y: 2, z: 4, core: 2. Of those that a mesh axis runs over, the one named last changes fastest.
Arguments:
- amplitudes: float32 [8, 512, 1024], P('wide', None, 'narrow'), may hold values from -6 to 6
- partner: float32 [64, 2048, 1024], P(None, 'wide', 'narrow'), may hold values from -0.1875 to 0.1875
- gate_block: float32 [8, 8], replicated, may hold values from -2 to 2
- slice_bits: int32 [6], replicated, may hold values from 0 to 1, as said below
- bit_order: int32 [9], replicated, may hold values from 0 to 8, each once
Outputs:
- contracted: float32 [8, 512, 2048], P(None, 'wide', 'narrow')
Inputs may be any that keep to these rules, and one draw needn't show every extreme that they name: bit_order is a permutation of 0 to 8. `slice_bits`: each entry is 0 or 1; the bits are never all equal.
All inputs are finite; a program needn't handle non-finite values.
Results may differ from a plain program's by a relative error of at most 0.00007.
Values sent between devices are 32-bit elements; how exact they have to be, the bound alone decides.
A program may use at most 64 MiB of HBM per device.

v0:
```python
import jax
import jax.numpy as jnp
from jax import lax
from jax.sharding import PartitionSpec as P


def source_rows(bit_order, total_rows):
    width = bit_order.shape[0]
    row_ids = jnp.arange(total_rows, dtype=jnp.int32)
    picked = jnp.bitwise_and(jnp.right_shift(row_ids[:, None], bit_order[None, :]), 1)
    powers = jnp.left_shift(jnp.ones((width,), jnp.int32), jnp.arange(width, dtype=jnp.int32))
    return jnp.sum(picked * powers[None, :], axis=1)


def slice_number(slice_bits):
    width = slice_bits.shape[0]
    powers = jnp.left_shift(jnp.ones((width,), jnp.int32), jnp.arange(width, dtype=jnp.int32))
    return jnp.sum(slice_bits * powers)


def contract_partner(left_rows, chosen):
    partial_terms = lax.dot_general(
        left_rows,
        lax.all_gather(chosen, "wide", axis=0, tiled=True),
        (((1,), (1,)), ((), ())),
        precision=lax.Precision.HIGHEST,
        preferred_element_type=jnp.float32,
    )
    return lax.psum_scatter(partial_terms, "narrow", scatter_dimension=1, tiled=True)


def gate_apply(gate_block, received):
    return jnp.einsum("qh,hlc->qlc", gate_block, received, precision=lax.Precision.HIGHEST)


def per_device(amplitudes, partner, gate_block, slice_bits, bit_order):
    source = source_rows(bit_order, amplitudes.shape[1])
    reordered = jnp.take(amplitudes[0], source, axis=0)
    chosen = lax.dynamic_index_in_dim(partner, slice_number(slice_bits), 0, keepdims=False)
    mixed = gate_apply(
        gate_block, lax.all_to_all(reordered[None], "wide", split_axis=1, concat_axis=0, tiled=True)
    )
    out_bits = mixed.shape[0]
    local_rows = mixed.shape[1]
    owned_part = contract_partner(mixed.reshape(out_bits * local_rows, mixed.shape[2]), chosen)
    return owned_part.reshape(out_bits, local_rows, owned_part.shape[1])


def solution(mesh):
    placed = (P("wide", None, "narrow"), P(None, "wide", "narrow"), P(), P(), P())
    return jax.shard_map(
        per_device, mesh=mesh, in_specs=placed, out_specs=P(None, "wide", "narrow"), check_vma=False
    )
```

profile of v0, /device:TPU:0, one launch (start us, length us, event | category | flops | bytes accessed | tf_op | source)
XLA Modules:
  0.0 127.9 jit_solution(4080367930417074534)
XLA Ops:
  6.5 0.0 copy-start
  6.5 0.0 all-gather.3.cloned.1.call-start
  6.5 1.4 %multiply_reduce_fusion.1 = s32[]{:T(128)} fusion(s32[6]{0:T(128)} %param.8), kind=kLoop, calls=%fused_computation.12 | loop fusion | flops 17 | bytes 28 | tf_op jit(solution)/shard_map/reduce_sum | solution.py:18
  9.8 1.7 %constant_dynamic-slice_fusion = f32[1,256,256]{2,1,0:T(8,128)} fusion(f32[64,256,256]{2,1,0:T(8,128)} %param.6, s32[]{:T(128)S(6)} %select_n.34), kind=kLoop, calls=%fused_computation.14 | loop fusion | bytes 524292 | tf_op jit(solution)/shard_map/jit(dynamic_index_in_dim)/dynamic_slice | solution.py:39
  11.5 0.0 all-gather.3.cloned.1.call-update
  11.5 0.0 reduce-scatter.2.cloned.1.call-start
  11.6 0.7 multiply_reduce_fusion
  12.4 0.0 copy-done
  12.4 0.0 copy-start.1
  12.4 1.6 %gather_fusion = f32[512,256]{1,0:T(8,128)S(1)} fusion(f32[512,256]{1,0:T(8,128)S(1)} %bitcast.17, s32[1024]{0:T(1024)S(1)} %pad_clamp_fusion), kind=kCustom, calls=%fused_computation | custom fusion | bytes 1050624 | tf_op jit(solution)/shard_map/jit(_take)/gather | solution.py:38
  14.0 0.1 bitcast_select_fusion
  14.1 0.5 copy.11
  14.7 30.0 %all_to_all.12 = f32[1,512,256]{2,0,1:T(1,128)S(1)} all-to-all(f32[1,512,256]{2,0,1:T(1,128)S(1)} %copy.11), channel_id=1, replica_groups=mesh['wide'=8,'narrow'=4] {'wide'}, dimensions={1} | all-to-all | bytes 1048576 | tf_op jit(solution)/shard_map/all_to_all | solution.py:41
  44.7 0.0 copy-done.1
  44.8 0.9 convolution_bitcast_fusion
  45.6 0.2 copy.13
  45.8 25.3 %all-gather.3.cloned.1.call-done = f32[1,2048,256]{2,1,0:T(8,128)} async-done(((f32[1,256,256]{2,1,0:T(8,128)}), f32[1,2048,256]{2,1,0:T(8,128)}) %all-gather.3.cloned.1.call-update) | async-done | bytes 2097168 | tf_op jit(solution)/shard_map/all_gather | solution.py:24
  71.1 6.7 %fusion = f32[512,2048]{1,0:T(8,128)} fusion(f32[512,256]{1,0:T(8,128)S(1)} %bitcast.19, f32[1,2048,256]{2,1,0:T(8,128)} %all-gather.3.cloned.1.call-done), kind=kOutput, calls=%fused_computation.1 | convolution fusion | flops 3221225472 | bytes 6815744 | tf_op jit(solution)/shard_map/dot_general | solution.py:22
  77.8 0.0 reduce-scatter.2.cloned.1.call-update
  77.9 43.2 %reduce-scatter.2.cloned.1.call-done = f32[512,512]{1,0:T(8,128)} async-done(((f32[512,2048]{1,0:T(8,128)}), f32[512,512]{1,0:T(8,128)}) %reduce-scatter.2.cloned.1.call-update) | async-done | bytes 1048592 | tf_op jit(solution)/shard_map/reduce_scatter | solution.py:29
  (5 shorter events, 0.1 us)
Async XLA Ops:
  6.5 5.8 %copy-start = (f32[1,512,256]{2,1,0:T(8,128)S(1)}, f32[1,512,256]{2,1,0:T(8,128)}, u32[]{:S(2)}) copy-start(f32[1,512,256]{2,1,0:T(8,128)} %param.5) | copy-start | bytes 1572868
  6.5 64.5 %all-gather.3.cloned.1.call-start = ((), (), s32[]{:S(2)}) async-start(), calls=%async_computation.3 | async-start | bytes 2359296 | tf_op jit(solution)/shard_map/all_gather | solution.py:24
  11.5 109.5 %reduce-scatter.2.cloned.1.call-start = ((), (), s32[]{:S(2)}) async-start(), calls=%async_computation.2 | async-start | bytes 5242880 | tf_op jit(solution)/shard_map/reduce_scatter | solution.py:29
  12.4 32.4 %copy-start.1 = (f32[8,8]{1,0:T(8,128)S(1)}, f32[8,8]{1,0:T(8,128)}, u32[]{:S(2)}) copy-start(f32[8,8]{1,0:T(8,128)} %param.7) | copy-start | bytes 772
Sparse Core Ops, SparseCore 0:
  11.7 59.3 all-gather.2
  78.0 43.0 reduce-scatter.1
where the time goes:
time: 128 us
  waiting for transfers between devices  68.5 us (54%)
  blocking collectives  30 us (23%)
  between operations  15.4 us (12%)
  matrix products  7.63 us (6%)
  local copies, waits for them, and re-layouts  4 us (3%)
  other arithmetic  2.26 us (2%)
    reduce_scatter x1, waiting for transfers between devices, contract_partner(): lax.psum_scatter(partial_terms, 'narrow', scatter_dimension=1, tiled=True)  43.2 us
    all_to_all x1, blocking collectives, per_device(): lax.all_to_all(reordered[None], 'wide', split_axis=1, concat_axis=0, tile...  30 us
    all_gather x1, waiting for transfers between devices, contract_partner(): lax.all_gather(chosen, 'wide', axis=0, tiled=True)  25.3 us
    dot_general x1, matrix products, contract_partner(): lax.dot_general(left_rows, lax.all_gather(chosen, 'wide', axis=0, tiled=T...  6.75 us
  transfers between devices with their start and end apart: 2, of which 2 were waited for; matrix products, arithmetic and copies ran while one was open for 3% of the time, Pallas kernels for 0%

commit v1 on v0

--- a/solution.py
+++ b/solution.py
@@ -2,6 +2,27 @@
 import jax.numpy as jnp
 from jax import lax
 from jax.sharding import PartitionSpec as P
+
+
+def ring_gather(x, axis, dim):
+    length, index, extent = (lax.axis_size(axis), lax.axis_index(axis), x.shape[dim])
+    forward = [(i, (i + 1) % length) for i in range(length)]
+    behind = [(i, (i - 1) % length) for i in range(length)]
+    out = jnp.zeros((*x.shape[:dim], length * extent, *x.shape[dim + 1 :]), x.dtype)
+    out = lax.dynamic_update_slice_in_dim(out, x, index * extent, axis=dim)
+    from_left = from_right = x
+    half = length // 2
+    for step in range(1, half + 1):
+        from_left = lax.ppermute(from_left, axis, forward)
+        out = lax.dynamic_update_slice_in_dim(
+            out, from_left, (index - step) % length * extent, axis=dim
+        )
+        if step < length - half:
+            from_right = lax.ppermute(from_right, axis, behind)
+            out = lax.dynamic_update_slice_in_dim(
+                out, from_right, (index + step) % length * extent, axis=dim
+            )
+    return out
 
 
 def source_rows(bit_order, total_rows):
@@ -21,7 +42,7 @@
 def contract_partner(left_rows, chosen):
     partial_terms = lax.dot_general(
         left_rows,
-        lax.all_gather(chosen, "wide", axis=0, tiled=True),
+        ring_gather(chosen, "wide", 0),
         (((1,), (1,)), ((), ())),
         precision=lax.Precision.HIGHEST,
         preferred_element_type=jnp.float32,

time: 128 us -> 123 us (0.961)
  blocking collectives: 30 us -> 0 us
  starting transfers between devices: 0.04 us -> 23.9 us
  local copies, waits for them, and re-layouts: 4 us -> 8.95 us
  matrix products: 7.63 us -> 6.02 us
  waiting for transfers between devices: 68.5 us -> 66.9 us
    all_to_all x1 -> x0, blocking collectives: 30 us -> none  [per_device(): lax.all_to_all(reordered[None], 'wide', split_axis=1, concat_axis=0, tile...]
    all_gather x1 -> x0, waiting for transfers between devices: 25.3 us -> none  [contract_partner(): lax.all_gather(chosen, 'wide', axis=0, tiled=True)]
    ppermute x0 -> x7, waiting for transfers between devices: none -> 23.5 us  [the longest x4 23.5 us: ring_gather(): from_left = lax.ppermute(from_left, axis, forward)]
    ppermute x0 -> x7, starting transfers between devices: none -> 20.3 us  [the longest x4 11 us: ring_gather(): from_left = lax.ppermute(from_left, axis, forward)]
    dynamic_update_slice x0 -> x8, local copies, waits for them, and re-layouts: none -> 5.69 us  [the longest x4 2.97 us: ring_gather(): lax.dynamic_update_slice_in_dim(out, from_left, (index - step) % length *...]
    all_to_all x0 -> x1, starting transfers between devices: none -> 3.49 us  [per_device(): lax.all_to_all(reordered[None], 'wide', split_axis=1, concat_axis=0, tile...]
    dynamic_slice x1 -> x0, local copies, waits for them, and re-layouts: 1.67 us -> none  [per_device(): lax.dynamic_index_in_dim(partner, slice_number(slice_bits), 0, keepdims=F...]
    dot_general x1, matrix products: 6.75 us -> 5.13 us  [contract_partner(): lax.dot_general(left_rows, ring_gather(chosen, 'wide', 0), (((1,), (1,)),...]
  transfers between devices with their start and end apart: 2 -> 9, of which waited for: 2 -> 5; matrix products, arithmetic and copies ran while one was open for 3% -> 7% of each run, Pallas kernels for 0% -> 0%
where the time goes in v1:
time: 123 us
  waiting for transfers between devices  66.9 us (54%)
  starting transfers between devices  23.9 us (19%)
  between operations  15.5 us (13%)
  local copies, waits for them, and re-layouts  8.95 us (7%)
  matrix products  6.02 us (5%)
  other arithmetic  1.61 us (1%)
    reduce_scatter x1, waiting for transfers between devices, contract_partner(): lax.psum_scatter(partial_terms, 'narrow', scatter_dimension=1, tiled=True)  43.4 us
    ppermute x4, waiting for transfers between devices, ring_gather(): from_left = lax.ppermute(from_left, axis, forward)  23.5 us
    ppermute x4, starting transfers between devices, ring_gather(): from_left = lax.ppermute(from_left, axis, forward)  11 us
    ppermute x3, starting transfers between devices, ring_gather(): from_right = lax.ppermute(from_right, axis, behind)  9.37 us
    dot_general x1, matrix products, contract_partner(): lax.dot_general(left_rows, ring_gather(chosen, 'wide', 0), (((1,), (1,)),...  5.13 us
    all_to_all x1, starting transfers between devices, per_device(): lax.all_to_all(reordered[None], 'wide', split_axis=1, concat_axis=0, tile...  3.49 us
    dynamic_update_slice x4, local copies, waits for them, and re-layouts, ring_gather(): lax.dynamic_update_slice_in_dim(out, from_left, (index - step) % length *...  2.97 us
  transfers between devices with their start and end apart: 9, of which 5 were waited for; matrix products, arithmetic and copies ran while one was open for 7% of the time, Pallas kernels for 0%

profile of v1, /device:TPU:0, one launch (start us, length us, event | category | flops | bytes accessed | tf_op | source)
XLA Modules:
  0.0 122.9 jit_solution(12099227773220351822)
XLA Ops:
  6.5 1.4 %multiply_reduce_fusion.1 = s32[]{:T(128)} fusion(s32[6]{0:T(128)} %param.8), kind=kLoop, calls=%fused_computation.19 | loop fusion | flops 17 | bytes 28 | tf_op jit(solution)/shard_map/reduce_sum | solution.py:39
  9.8 0.1 broadcast_in_dim.19
  10.0 1.7 %constant_dynamic-update-slice_fusion.7 = (f32[2048,256]{1,0:T(8,128)S(1)}, f32[256,256]{1,0:T(8,128)}) fusion(f32[2048,256]{1,0:T(8,128)S(1)} %broadcast_in_dim.19, s32[]{:T(128)S(6)} %select_n.90, f32[64,256,256]{2,1,0:T(8,128)} %param.6, s32[]{:T(128)S(6)} %select_n.89), kind=kLoop, calls=%fused_computation.17 | loop fusion | bytes 786440 | tf_op jit(solution)/shard_map/dynamic_update_slice | solution.py:12
  11.7 3.0 %collective-permute-start = (f32[256,256]{1,0:T(8,128)}, f32[256,256]{1,0:T(8,128)}, u32[]{:S(2)}, u32[]{:S(2)}) collective-permute-start(f32[256,256]{1,0:T(8,128)} %get-tuple-element.6), channel_id=1, source_target_pairs={{0,4},{4,8},{8,12},{12,16},{16,20},{20,24},{24,28},{28,0},{1,5},{5... | collective-permute-start | bytes 786440 | tf_op jit(solution)/shard_map/ppermute | solution.py:16
  14.7 3.0 %collective-permute-start.1 = (f32[256,256]{1,0:T(8,128)}, f32[256,256]{1,0:T(8,128)S(1)}, u32[]{:S(2)}, u32[]{:S(2)}) collective-permute-start(f32[256,256]{1,0:T(8,128)} %get-tuple-element.6), channel_id=1, source_target_pairs={{0,28},{4,0},{8,4},{12,8},{16,12},{20,16},{24,20},{28,24},{1,29},{... | collective-permute-start | bytes 786440 | tf_op jit(solution)/shard_map/ppermute | solution.py:21
  17.7 0.1 multiply_reduce_fusion
  17.8 1.6 %gather_fusion = f32[512,256]{1,0:T(8,128)S(1)} fusion(f32[512,256]{1,0:T(8,128)S(1)} %bitcast.18, s32[1024]{0:T(1024)S(1)} %pad_clamp_fusion), kind=kCustom, calls=%fused_computation | custom fusion | bytes 1050624 | tf_op jit(solution)/shard_map/jit(_take)/gather | solution.py:59
  19.4 0.1 bitcast_select_fusion
  19.6 1.3 %copy.11 = f32[1,512,256]{2,0,1:T(1,128)} copy(f32[1,512,256]{2,1,0:T(8,128)S(1)} %bitcast_select_fusion) | data formatting | bytes 1048576 | tf_op jit(solution)/shard_map/jit(_take)/select_n | solution.py:59
  20.9 3.5 %all-to-all-start = ((f32[1,512,256]{2,0,1:T(1,128)}), f32[1,512,256]{2,0,1:T(1,128)S(1)}, u32[]{:S(2)}, u32[]{:S(2)}) async-start(f32[1,512,256]{2,0,1:T(1,128)} %copy.11), calls=%async_computation | async-start | bytes 1048576 | tf_op jit(solution)/shard_map/all_to_all | solution.py:62
  24.4 0.0 reduce-scatter.2.cloned.1.call-start
  24.4 3.9 %collective-permute-done = f32[256,256]{1,0:T(8,128)} collective-permute-done((f32[256,256]{1,0:T(8,128)}, f32[256,256]{1,0:T(8,128)}, u32[]{:S(2)}, u32[]{:S(2)}) %collective-permute-start) | collective-permute-done | bytes 262176 | tf_op jit(solution)/shard_map/ppermute | solution.py:16
  28.3 3.7 %collective-permute-start.2 = (f32[256,256]{1,0:T(8,128)}, f32[256,256]{1,0:T(8,128)}, u32[]{:S(2)}, u32[]{:S(2)}) collective-permute-start(f32[256,256]{1,0:T(8,128)} %collective-permute-done), channel_id=1, source_target_pairs={{0,4},{4,8},{8,12},{12,16},{16,20},{20,24},{24,28},{28,0},{1,5},{5... | collective-permute-start | bytes 786440 | tf_op jit(solution)/shard_map/ppermute | solution.py:16
  32.0 3.2 %collective-permute-start.3 = (f32[256,256]{1,0:T(8,128)S(1)}, f32[256,256]{1,0:T(8,128)}, u32[]{:S(2)}, u32[]{:S(2)}) collective-permute-start(f32[256,256]{1,0:T(8,128)S(1)} %collective-permute-done.1), channel_id=1, source_target_pairs={{0,28},{4,0},{8,4},{12,8},{16,12},{20,16},{24,20},{28,24},{1,29},{... | collective-permute-start | bytes 786440 | tf_op jit(solution)/shard_map/ppermute | solution.py:21
  35.3 1.0 constant_dynamic-update-slice_fusion.6
  36.3 7.4 %collective-permute-done.2 = f32[256,256]{1,0:T(8,128)} collective-permute-done((f32[256,256]{1,0:T(8,128)}, f32[256,256]{1,0:T(8,128)}, u32[]{:S(2)}, u32[]{:S(2)}) %collective-permute-start.2) | collective-permute-done | bytes 262176 | tf_op jit(solution)/shard_map/ppermute | solution.py:16
  43.7 1.8 %collective-permute-start.4 = (f32[256,256]{1,0:T(8,128)}, f32[256,256]{1,0:T(8,128)}, u32[]{:S(2)}, u32[]{:S(2)}) collective-permute-start(f32[256,256]{1,0:T(8,128)} %collective-permute-done.2), channel_id=1, source_target_pairs={{0,4},{4,8},{8,12},{12,16},{16,20},{20,24},{24,28},{28,0},{1,5},{5... | collective-permute-start | bytes 786440 | tf_op jit(solution)/shard_map/ppermute | solution.py:16
  45.5 0.0 collective-permute-done.3
  45.5 3.1 %collective-permute-start.5 = (f32[256,256]{1,0:T(8,128)}, f32[256,256]{1,0:T(8,128)S(1)}, u32[]{:S(2)}, u32[]{:S(2)}) collective-permute-start(f32[256,256]{1,0:T(8,128)} %collective-permute-done.3), channel_id=1, source_target_pairs={{0,28},{4,0},{8,4},{12,8},{16,12},{20,16},{24,20},{28,24},{1,29},{... | collective-permute-start | bytes 786440 | tf_op jit(solution)/shard_map/ppermute | solution.py:21
  48.6 1.0 constant_dynamic-update-slice_fusion.4
  49.6 1.0 constant_dynamic-update-slice_fusion.3
  50.6 5.8 %collective-permute-done.4 = f32[256,256]{1,0:T(8,128)} collective-permute-done((f32[256,256]{1,0:T(8,128)}, f32[256,256]{1,0:T(8,128)}, u32[]{:S(2)}, u32[]{:S(2)}) %collective-permute-start.4) | collective-permute-done | bytes 262176 | tf_op jit(solution)/shard_map/ppermute | solution.py:16
  56.3 2.5 %collective-permute-start.6 = (f32[256,256]{1,0:T(8,128)}, f32[256,256]{1,0:T(8,128)S(1)}, u32[]{:S(2)}, u32[]{:S(2)}) collective-permute-start(f32[256,256]{1,0:T(8,128)} %collective-permute-done.4), channel_id=1, source_target_pairs={{0,4},{4,8},{8,12},{12,16},{16,20},{20,24},{24,28},{28,0},{1,5},{5... | collective-permute-start | bytes 786440 | tf_op jit(solution)/shard_map/ppermute | solution.py:16
  58.8 1.0 constant_dynamic-update-slice_fusion.2
  59.8 0.0 collective-permute-done.5
  59.9 0.0 all-to-all-done
  59.9 0.9 convolution_bitcast_fusion
  60.8 0.2 copy.13
  61.0 6.5 %collective-permute-done.6 = f32[256,256]{1,0:T(8,128)S(1)} collective-permute-done((f32[256,256]{1,0:T(8,128)}, f32[256,256]{1,0:T(8,128)S(1)}, u32[]{:S(2)}, u32[]{:S(2)}) %collective-permute-start.6) | collective-permute-done | bytes 262176 | tf_op jit(solution)/shard_map/ppermute | solution.py:16
  67.5 5.1 %fusion.2 = f32[512,2048]{1,0:T(8,128)} fusion(f32[512,256]{1,0:T(8,128)S(1)} %bitcast.20, f32[2048,256]{1,0:T(8,128)S(1)} %constant_dynamic-update-slice_fusion), kind=kOutput, calls=%fused_computation.21 | convolution fusion | flops 3221225472 | bytes 6815744 | tf_op jit(solution)/shard_map/dot_general | solution.py:43
  72.6 0.0 reduce-scatter.2.cloned.1.call-update
  72.7 43.4 %reduce-scatter.2.cloned.1.call-done = f32[512,512]{1,0:T(8,128)} async-done(((f32[512,2048]{1,0:T(8,128)}), f32[512,512]{1,0:T(8,128)}) %reduce-scatter.2.cloned.1.call-update) | async-done | bytes 1048592 | tf_op jit(solution)/shard_map/reduce_scatter | solution.py:50
  (15 shorter events, 0.1 us)
Async XLA Ops:
  6.5 11.3 %copy-start = (f32[1,512,256]{2,1,0:T(8,128)S(1)}, f32[1,512,256]{2,1,0:T(8,128)}, u32[]{:S(2)}) copy-start(f32[1,512,256]{2,1,0:T(8,128)} %param.5) | copy-start | bytes 1572868
  6.5 11.2 %copy-start.2 = (s32[9]{0:T(128)S(1)}, s32[9]{0:T(128)}, u32[]{:S(2)}) copy-start(s32[9]{0:T(128)} %param.9) | copy-start | bytes 112
  11.7 16.6 %collective-permute-start = (f32[256,256]{1,0:T(8,128)}, f32[256,256]{1,0:T(8,128)}, u32[]{:S(2)}, u32[]{:S(2)}) collective-permute-start(f32[256,256]{1,0:T(8,128)} %get-tuple-element.6), channel_id=1, source_target_pairs={{0,4},{4,8},{8,12},{12,16},{16,20},{20,24},{24,28},{28,0},{1,5},{5... | collective-permute-start | bytes 786440 | tf_op jit(solution)/shard_map/ppermute | solution.py:16
  14.7 17.4 %collective-permute-start.1 = (f32[256,256]{1,0:T(8,128)}, f32[256,256]{1,0:T(8,128)S(1)}, u32[]{:S(2)}, u32[]{:S(2)}) collective-permute-start(f32[256,256]{1,0:T(8,128)} %get-tuple-element.6), channel_id=1, source_target_pairs={{0,28},{4,0},{8,4},{12,8},{16,12},{20,16},{24,20},{28,24},{1,29},{... | collective-permute-start | bytes 786440 | tf_op jit(solution)/shard_map/ppermute | solution.py:21
  20.9 39.0 %all-to-all-start = ((f32[1,512,256]{2,0,1:T(1,128)}), f32[1,512,256]{2,0,1:T(1,128)S(1)}, u32[]{:S(2)}, u32[]{:S(2)}) async-start(f32[1,512,256]{2,0,1:T(1,128)} %copy.11), calls=%async_computation | async-start | bytes 1048576 | tf_op jit(solution)/shard_map/all_to_all | solution.py:62
  24.4 91.6 %reduce-scatter.2.cloned.1.call-start = ((), (), s32[]{:S(2)}) async-start(), calls=%async_computation.2 | async-start | bytes 5242880 | tf_op jit(solution)/shard_map/reduce_scatter | solution.py:50
  28.3 15.4 %collective-permute-start.2 = (f32[256,256]{1,0:T(8,128)}, f32[256,256]{1,0:T(8,128)}, u32[]{:S(2)}, u32[]{:S(2)}) collective-permute-start(f32[256,256]{1,0:T(8,128)} %collective-permute-done), channel_id=1, source_target_pairs={{0,4},{4,8},{8,12},{12,16},{16,20},{20,24},{24,28},{28,0},{1,5},{5... | collective-permute-start | bytes 786440 | tf_op jit(solution)/shard_map/ppermute | solution.py:16
  32.0 13.5 %collective-permute-start.3 = (f32[256,256]{1,0:T(8,128)S(1)}, f32[256,256]{1,0:T(8,128)}, u32[]{:S(2)}, u32[]{:S(2)}) collective-permute-start(f32[256,256]{1,0:T(8,128)S(1)} %collective-permute-done.1), channel_id=1, source_target_pairs={{0,28},{4,0},{8,4},{12,8},{16,12},{20,16},{24,20},{28,24},{1,29},{... | collective-permute-start | bytes 786440 | tf_op jit(solution)/shard_map/ppermute | solution.py:21
  35.3 24.6 %copy-start.1 = (f32[8,8]{1,0:T(8,128)S(1)}, f32[8,8]{1,0:T(8,128)}, u32[]{:S(2)}) copy-start(f32[8,8]{1,0:T(8,128)} %param.7) | copy-start | bytes 772
  43.7 12.6 %collective-permute-start.4 = (f32[256,256]{1,0:T(8,128)}, f32[256,256]{1,0:T(8,128)}, u32[]{:S(2)}, u32[]{:S(2)}) collective-permute-start(f32[256,256]{1,0:T(8,128)} %collective-permute-done.2), channel_id=1, source_target_pairs={{0,4},{4,8},{8,12},{12,16},{16,20},{20,24},{24,28},{28,0},{1,5},{5... | collective-permute-start | bytes 786440 | tf_op jit(solution)/shard_map/ppermute | solution.py:16
  45.5 14.3 %collective-permute-start.5 = (f32[256,256]{1,0:T(8,128)}, f32[256,256]{1,0:T(8,128)S(1)}, u32[]{:S(2)}, u32[]{:S(2)}) collective-permute-start(f32[256,256]{1,0:T(8,128)} %collective-permute-done.3), channel_id=1, source_target_pairs={{0,28},{4,0},{8,4},{12,8},{16,12},{20,16},{24,20},{28,24},{1,29},{... | collective-permute-start | bytes 786440 | tf_op jit(solution)/shard_map/ppermute | solution.py:21
  56.3 11.1 %collective-permute-start.6 = (f32[256,256]{1,0:T(8,128)}, f32[256,256]{1,0:T(8,128)S(1)}, u32[]{:S(2)}, u32[]{:S(2)}) collective-permute-start(f32[256,256]{1,0:T(8,128)} %collective-permute-done.4), channel_id=1, source_target_pairs={{0,4},{4,8},{8,12},{12,16},{16,20},{20,24},{24,28},{28,0},{1,5},{5... | collective-permute-start | bytes 786440 | tf_op jit(solution)/shard_map/ppermute | solution.py:16
Sparse Core Ops, SparseCore 0:
  72.8 43.2 reduce-scatter.1
